TPU v7x, 256 devices: a whole 4x4x8 slice. The times are simulated.
256 devices in a mesh: frames: 16 (over z, core), rows: 16 (over y, x).
Axes of the slice: x: 4, y: 4, z: 8, core: 2. Of those that a mesh axis runs over, the one named last changes fastest.
Arguments:
- observed: bfloat16 [64, 1, 256, 2048], P('frames', None, 'rows'), may hold values from -6 to 6
- history: bfloat16 [127, 1, 256, 2048], P(None, None, 'rows', 'frames'), may hold values from 0 to 0.3984375
- spikes_start: float32 [64, 1, 256, 2048], P('frames', None, 'rows'), may hold values from 0 to 0.4
- kernel: bfloat16 [128], replicated, may hold values from 0 to 1, as said below
- smooth_half: float32 [8], replicated, may hold values from 0.2 to 1
Outputs:
- spikes: float32 [64, 1, 256, 2048], P('frames', None, 'rows')
- point: float32 [64, 1, 256, 2048], P('frames', None, 'rows')
Inputs may be any that keep to these rules, and one draw needn't show every extreme that they name: kernel taps are positive and fall roughly exponentially over the lags.
All inputs are finite; a program needn't handle non-finite values.
Results may differ from a plain program's by a relative error of at most 0.0012.
The roundings to bfloat16 on the way count: a program that leaves them out, or rounds other values in their place, can miss the bound.
Values may be sent and summed in bfloat16 or wider, within the bound.
A program may use at most 64 MiB of HBM per device.

v0:
```python
import functools
import math

import jax
import jax.numpy as jnp
from jax import lax
from jax.experimental import pallas as pl
from jax.experimental.pallas import tpu as pltpu
from jax.sharding import PartitionSpec as P

ITERS = 2
REG_WEIGHT = 4.0
SPARSE_WEIGHT = 0.1
MESH = pl.DeviceIdType.MESH
F32 = jnp.float32
BF16 = jnp.bfloat16
GROUPS = 8


def momentum_terms(count):
    current = 1.0
    terms = []
    for iteration in range(count):
        upcoming = (1.0 + math.sqrt(1.0 + 4.0 * current * current)) / 2.0
        terms.append((current - 1.0) / upcoming)
        current = upcoming
    return terms


def iota(shape, dim):
    return lax.broadcasted_iota(jnp.int32, shape, dim)


def dot(a, b):
    return jnp.dot(a, b, preferred_element_type=F32)


def onehot(cond):
    return jnp.where(cond, 1.0, 0.0).astype(BF16)


def split(value):
    high = value.astype(BF16)
    return high, (value - high.astype(F32)).astype(BF16)


def body(
    nf,
    nr,
    frames,
    obs_hbm,
    hist_hbm,
    start_hbm,
    taps_ref,
    half_ref,
    out_spikes,
    out_point,
    start_f,
    hi_f,
    lo_f,
    hi_c,
    lo_c,
    obs_c,
    hist_v,
    grad_c,
    grad_f,
    edge_s,
    strip_s,
    above,
    below,
    strips,
    row_s,
    row_r,
    kh,
    kw,
    kwt,
    band,
    ah,
    al,
    sel,
    hbh,
    hbl,
    local_sems,
    a2a_send,
    a2a_recv,
    halo_send,
    halo_recv,
    sum_send,
    sum_recv,
):
    col = lax.axis_index("frames")
    row = lax.axis_index("rows")
    per = frames // nf
    rows = frames * 8
    hist_len = hist_hbm.shape[0]
    tap_count = taps_ref.shape[1]

    load_start = pltpu.make_async_copy(start_hbm, start_f, local_sems.at[0])
    load_start.start()
    load_hist = pltpu.make_async_copy(hist_hbm, hist_v.at[pl.ds(0, hist_len)], local_sems.at[1])
    load_hist.start()

    above[...] = jnp.zeros(above.shape, BF16)
    below[...] = jnp.zeros(below.shape, BF16)
    strips[...] = jnp.zeros(strips.shape, BF16)
    hist_v[hist_len:] = jnp.zeros((hist_v.shape[0] - hist_len,) + hist_v.shape[1:], BF16)

    barrier = pltpu.get_barrier_semaphore()

    def signal_frames(k, carry):
        pl.semaphore_signal(
            barrier, inc=1, device_id={"frames": lax.rem(col + k, nf)}, device_id_type=MESH
        )
        return carry

    def signal_rows(k, carry):
        pl.semaphore_signal(
            barrier, inc=1, device_id={"rows": lax.rem(row + k, nr)}, device_id_type=MESH
        )
        return carry

    lax.fori_loop(1, nf, signal_frames, 0)
    lax.fori_loop(1, nr, signal_rows, 0)
    exists = {}
    for dc in (-1, 0, 1):
        for dr in (-1, 0, 1):
            conds = []
            if dc == -1:
                conds.append(col > 0)
            if dc == 1:
                conds.append(col < nf - 1)
            if dr == -1:
                conds.append(row > 0)
            if dr == 1:
                conds.append(row < nr - 1)
            if conds:
                exists[dc, dr] = functools.reduce(jnp.logical_and, conds)
    for dc in (-1, 1):
        for dr in (-1, 1):

            @pl.when(exists[dc, dr])
            def _():
                pl.semaphore_signal(
                    barrier,
                    inc=1,
                    device_id={"frames": col + dc, "rows": row + dr},
                    device_id_type=MESH,
                )

    load_start.wait()
    for c in range(nf):
        high, low = split(start_f[:, :, :, c * 128 : (c + 1) * 128])
        hi_f[c] = high
        lo_f[c] = low

    sides = (col > 0).astype(jnp.int32) + (col < nf - 1).astype(jnp.int32)
    ends = (row > 0).astype(jnp.int32) + (row < nr - 1).astype(jnp.int32)
    pl.semaphore_wait(barrier, (nf - 1) + (nr - 1) + sides * ends)

    def order(k):
        return nf // 2 + ((k + 1) // 2) * (1 - 2 * lax.rem(k, 2))

    def exchange(index, source, target, own_source, own_target):
        own = pltpu.make_async_copy(own_source, own_target, a2a_recv.at[index])
        own.start()

        def send(k, carry):
            peer = lax.rem(col + order(k), nf)
            pltpu.make_async_remote_copy(
                src_ref=source(peer),
                dst_ref=target,
                send_sem=a2a_send.at[index],
                recv_sem=a2a_recv.at[index],
                device_id={"frames": peer},
                device_id_type=MESH,
            ).start()
            return carry

        lax.fori_loop(0, nf - 1, send, 0)

    def wait_bytes(view, sem):
        pltpu.make_async_copy(view, view, sem).wait()

    def to_block(index, source, buffer):
        target = buffer.at[pl.ds(col * per, per)]
        exchange(index, source, target, source(col), target)

    to_block(0, lambda c: hi_f.at[c], hi_c)
    to_block(1, lambda c: obs_hbm.at[:, :, :, pl.ds(pl.multiple_of(c * 128, 128), 128)], obs_c)
    to_block(2, lambda c: lo_f.at[c], lo_c)

    def gradient_out(it):
        target = grad_f.at[it, col]
        exchange(
            3 + it,
            lambda f: grad_c.at[it, pl.ds(f * per, per)],
            target,
            grad_c.at[it, pl.ds(col * per, per)],
            target,
        )

    size = 256
    spread = jnp.concatenate(
        [taps_ref[...].astype(F32), jnp.zeros((1, size - tap_count), F32)], axis=1
    )
    spread = jnp.broadcast_to(spread, (size, size))
    shifted = pltpu.roll(spread, size - (tap_count - 1), 1, stride=1, stride_axis=0).astype(BF16)
    at_t = onehot(iota((rows, size), 0) // 8 == iota((rows, size), 1))
    by_s = lax.dot_general(
        at_t, shifted, (((1,), (1,)), ((), ())), preferred_element_type=F32
    ).astype(BF16)

    def same_row(shape):
        return lax.rem(iota(shape, 0), 8) == lax.rem(iota(shape, 1), 8)

    hist_cols = kh.shape[1]
    s_of = iota((size, hist_cols), 0)
    pick = onehot((s_of == iota((size, hist_cols), 1) // 8) & (s_of < hist_len))
    kh[...] = jnp.where(same_row((rows, hist_cols)), dot(by_s, pick), 0.0).astype(BF16)
    pick = onehot(iota((size, rows), 0) == iota((size, rows), 1) // 8 + hist_len)
    kw[...] = jnp.where(same_row((rows, rows)), dot(by_s, pick), 0.0).astype(BF16)
    at_s = onehot(iota((rows, size), 0) // 8 + hist_len == iota((rows, size), 1))
    by_t = dot(at_s, shifted).astype(BF16)
    pick = onehot(iota((size, rows), 0) == iota((size, rows), 1) // 8)
    kwt[...] = jnp.where(same_row((rows, rows)), dot(by_t, pick), 0.0).astype(BF16)

    half = [half_ref[k] for k in range(half_ref.shape[0])]
    reach = half_ref.shape[0] - 1
    total = half[0]
    for k in range(1, reach + 1):
        total = total + 2.0 * half[k]
    total = jnp.full((1, 1), total, F32)
    scale = 1.0 / (total * total)

    def taps_at(distance):
        value = jnp.zeros(distance.shape, F32)
        for k in range(reach + 1):
            value = jnp.where(distance == k, half[k], value)
        return value

    high, low = split(taps_at(jnp.abs(iota((128, 128), 0) - iota((128, 128), 1))))
    band[:, 0:128] = high
    band[:, 128:256] = low

    rg = ah.shape[0]
    i0, i1 = iota((rg, rg), 0), iota((rg, rg), 1)
    for d in (-1, 0, 1):
        near = taps_at(jnp.abs(8 * d + lax.rem(i1, 8) - lax.rem(i0, 8)))
        high, low = split(jnp.where(i0 // 8 == i1 // 8, near, 0.0))
        ah[:, (d + 1) * rg : (d + 2) * rg] = high
        al[:, (d + 1) * rg : (d + 2) * rg] = low

    k0, k1 = iota((256, 256), 0), iota((256, 256), 1)
    place = lax.rem(k0, 128)
    inner, line = lax.rem(place, 8), lax.rem(k1, 128)
    near = taps_at(jnp.where(k0 < 128, line + 8 - inner, 128 + inner - line))
    near = jnp.where(lax.rem(place // 8, 2) == k1 // 128, near, 0.0)
    for g in range(GROUPS):
        high, low = split(jnp.where(place // 16 == g, near, 0.0))
        hbh[:, g * 256 : (g + 1) * 256] = high
        hbl[:, g * 256 : (g + 1) * 256] = low
    place = lax.rem(k1, 128)
    inner, line = lax.rem(place, 8), lax.rem(k0, 128)
    chosen = (lax.rem(place // 8, 2) == k0 // 128) & (line == jnp.where(k1 < 128, 120 + inner, inner))
    for g in range(GROUPS):
        sel[g * 256 : (g + 1) * 256, :] = onehot(chosen & (place // 16 == g))

    def halves(ref):
        parts = [ref[:, h].astype(F32).reshape(rows, 128) for h in (0, 1)]
        return jnp.concatenate(parts, axis=1)

    load_hist.wait()
    past = [hist_v[:, h].astype(F32).reshape(hist_cols, 128) for h in (0, 1)]
    past = dot(kh[...], jnp.concatenate(past, axis=1).astype(BF16))

    chunk = rows // GROUPS

    def halo_copies(n):
        copies = [
            ((0, -1), edge_s.at[n, 0], below.at[n], 1),
            ((0, 1), edge_s.at[n, 1], above.at[n], 0),
        ]
        for dc in (-1, 1):
            side = 0 if dc == 1 else 1
            for dr in (-1, 0, 1):
                copies.append(
                    (
                        (dc, dr),
                        strip_s.at[n, side],
                        strips.at[n, 1 - dr, :, pl.ds(side * 128, 128)],
                        2 + side * 3 + 1 - dr,
                    )
                )
        return [
            (
                where,
                pltpu.make_async_remote_copy(
                    src_ref=source,
                    dst_ref=target,
                    send_sem=halo_send.at[n, slot],
                    recv_sem=halo_recv.at[n, slot],
                    device_id={"frames": col + where[0], "rows": row + where[1]},
                    device_id_type=MESH,
                ),
            )
            for where, source, target, slot in copies
        ]

    def halo_start(n, field):
        edge_s[n, 0] = field[:, 0:128]
        edge_s[n, 1] = field[:, 128:256]
        wide = [field[g * chunk : (g + 1) * chunk, :] for g in range(GROUPS)]
        packed = dot(jnp.concatenate(wide, axis=1), sel[...]).astype(BF16)
        strip_s[n, 0] = packed[:, 0:128]
        strip_s[n, 1] = packed[:, 128:256]
        for where, copy in halo_copies(n):

            @pl.when(exists[where])
            def _():
                copy.start()

    def halo_wait(n):
        for where, copy in halo_copies(n):

            @pl.when(exists[-where[0], -where[1]])
            def _():
                copy.wait_recv()

    def smooth(n, field):
        stacked = jnp.concatenate(
            [above[n], field[:, 0:128], field[:, 128:256], below[n]], axis=0
        )
        wide = dot(stacked, band[...])
        flat = wide[:, 0:128] + wide[:, 128:256]
        lines = strips[n].reshape(3 * chunk, 256)
        corner = dot(lines, hbh[...]) + dot(lines, hbl[...])

        def part(block, which, h):
            extra = [
                corner[which * chunk : (which + 1) * chunk, g * 256 + h * 128 : g * 256 + h * 128 + 128]
                for g in range(GROUPS)
            ]
            return flat[block * rows : (block + 1) * rows] + jnp.concatenate(extra, axis=0)

        blocks = [part(0, 0, 1), part(1, 1, 0), part(2, 1, 1), part(3, 2, 0)]
        pairs = [split(b) for b in blocks]
        result = []
        for q in range(rows // rg):
            cut = slice(q * rg, (q + 1) * rg)

            def tower(which):
                return jnp.concatenate(
                    [
                        jnp.concatenate([pairs[d][which][cut], pairs[d + 1][which][cut]], axis=1)
                        for d in range(3)
                    ],
                    axis=0,
                )

            high, low = tower(0), tower(1)
            result.append(dot(ah[...], high) + dot(ah[...], low) + dot(al[...], high))
        return jnp.concatenate(result, axis=0) * scale

    lane = iota((1, 128), 1)

    def reduce_over(it, stage, axis, count, me, value):
        row_s[it, stage] = value
        row_r[it, stage, pl.ds(me, 1)] = value.reshape(1, 1, 128)

        def send(k, carry):
            pltpu.make_async_remote_copy(
                src_ref=row_s.at[it, stage],
                dst_ref=row_r.at[it, stage, me],
                send_sem=sum_send.at[it, stage],
                recv_sem=sum_recv.at[it, stage],
                device_id={axis: lax.rem(me + k, count)},
                device_id_type=MESH,
            ).start()
            return carry

        lax.fori_loop(1, count, send, 0)
        wait_bytes(row_r.at[it, stage, pl.ds(0, count - 1)], sum_recv.at[it, stage])
        return jnp.sum(row_r[it, stage], axis=0)

    def step_size(it, norm, conv, curv):
        value = jnp.where(lane == 0, norm, jnp.where(lane == 1, conv, curv))
        value = reduce_over(it, 0, "frames", nf, col, value)
        value = reduce_over(it, 1, "rows", nr, row, value)
        return value[:, 0:1] / (value[:, 1:2] + REG_WEIGHT * value[:, 2:3])

    def total_of(value):
        return jnp.sum(value, keepdims=True)

    wait_bytes(hi_c, a2a_recv.at[0])
    point_bf = halves(hi_c).astype(BF16)
    halo_start(0, point_bf)
    seen = None
    steps = []
    for it in range(ITERS):
        now = dot(kw[...], point_bf)
        if it == 0:
            wait_bytes(obs_c, a2a_recv.at[1])
            past = past - halves(obs_c)
        resid_bf = (past + now).astype(BF16)
        back = dot(kwt[...], resid_bf).astype(BF16).astype(F32)
        halo_wait(2 * it)
        point_f = point_bf.astype(F32)
        gradient = back + REG_WEIGHT * (point_f - smooth(2 * it, point_bf))
        for h in (0, 1):
            grad_c[it, :, h] = gradient[:, h * 128 : (h + 1) * 128].reshape(frames, 8, 128)
        grad_bf = gradient.astype(BF16)
        halo_start(2 * it + 1, grad_bf)
        gradient_out(it)
        conv = dot(kw[...], grad_bf)
        norm, conv = total_of(gradient * gradient), total_of(conv * conv)
        halo_wait(2 * it + 1)
        grad_smooth = smooth(2 * it + 1, grad_bf)
        grad_f32 = grad_bf.astype(F32)
        curv = total_of(grad_f32 * (grad_f32 - grad_smooth))
        step = step_size(it, norm, conv, curv)
        steps.append(step)
        if it == 0:
            wait_bytes(lo_c, a2a_recv.at[2])
            point = halves(hi_c) + halves(lo_c)
            point = jnp.maximum(point - step * gradient - step * SPARSE_WEIGHT, 0.0)
            point_bf = point.astype(BF16)
            halo_start(2, point_bf)

    betas = momentum_terms(ITERS)
    for it in range(ITERS):
        wait_bytes(grad_f.at[it], a2a_recv.at[3 + it])
    for c in range(nf):
        cut = slice(c * 128, (c + 1) * 128)
        previous = start_f[:, :, :, cut]
        point = previous
        for it in range(ITERS):
            step = steps[it].reshape(1, 1, 1, 1)
            updated = jnp.maximum(
                point - step * grad_f[it, c] - step * SPARSE_WEIGHT, 0.0
            )
            point = updated + betas[it] * (updated - previous) if betas[it] else updated
            previous = updated
        out_spikes[:, :, :, cut] = previous
        out_point[:, :, :, cut] = point

    wait_bytes(hi_f.at[pl.ds(0, nf - 1)], a2a_send.at[0])
    wait_bytes(obs_c.at[pl.ds(0, per * (nf - 1))], a2a_send.at[1])
    wait_bytes(lo_f.at[pl.ds(0, nf - 1)], a2a_send.at[2])
    for it in range(ITERS):
        wait_bytes(grad_f.at[it, pl.ds(0, nf - 1)], a2a_send.at[3 + it])
        for stage, count in ((0, nf), (1, nr)):
            wait_bytes(row_r.at[it, stage, pl.ds(0, count - 1)], sum_send.at[it, stage])
        for n in (2 * it, 2 * it + 1):
            for where, copy in halo_copies(n):

                @pl.when(exists[where])
                def _():
                    copy.wait_send()


def shards(nf, nr, observed, history, spikes_start, kernel, smooth_half):
    per, _, tall, cols = observed.shape
    frames = per * nf
    rows = frames * 8
    hist = history.shape[0]
    assert tall == 16 and history.shape[3] == 128 and cols == 128 * nf
    hist_pad = hist + 1
    rg = min(rows, 256)
    chunk = rows // GROUPS
    most = max(nf, nr)
    block = (per, 2, 8, 128)
    any_spec = pl.BlockSpec(memory_space=pl.ANY)
    vmem = pl.BlockSpec(memory_space=pltpu.VMEM)
    out = jax.ShapeDtypeStruct((per, 2, 8, cols), F32)
    spikes, point = pl.pallas_call(
        functools.partial(body, nf, nr, frames),
        out_shape=(out, out),
        in_specs=[any_spec, any_spec, any_spec, vmem, pl.BlockSpec(memory_space=pltpu.SMEM)],
        out_specs=(vmem, vmem),
        scratch_shapes=[
            pltpu.VMEM((per, 2, 8, cols), F32),
            pltpu.VMEM((nf,) + block, BF16),
            pltpu.VMEM((nf,) + block, BF16),
            pltpu.VMEM((frames, 2, 8, 128), BF16),
            pltpu.VMEM((frames, 2, 8, 128), BF16),
            pltpu.VMEM((frames, 2, 8, 128), BF16),
            pltpu.VMEM((hist_pad, 2, 8, 128), BF16),
            pltpu.VMEM((ITERS, frames, 2, 8, 128), F32),
            pltpu.VMEM((ITERS, nf) + block, F32),
            pltpu.VMEM((2 * ITERS, 2, rows, 128), BF16),
            pltpu.VMEM((2 * ITERS, 2, chunk, 128), BF16),
            pltpu.VMEM((2 * ITERS, rows, 128), BF16),
            pltpu.VMEM((2 * ITERS, rows, 128), BF16),
            pltpu.VMEM((2 * ITERS, 3, chunk, 256), BF16),
            pltpu.VMEM((ITERS, 2, 1, 128), F32),
            pltpu.VMEM((ITERS, 2, most, 1, 128), F32),
            pltpu.VMEM((rows, 8 * hist_pad), BF16),
            pltpu.VMEM((rows, rows), BF16),
            pltpu.VMEM((rows, rows), BF16),
            pltpu.VMEM((128, 256), BF16),
            pltpu.VMEM((rg, 3 * rg), BF16),
            pltpu.VMEM((rg, 3 * rg), BF16),
            pltpu.VMEM((GROUPS * 256, 256), BF16),
            pltpu.VMEM((256, GROUPS * 256), BF16),
            pltpu.VMEM((256, GROUPS * 256), BF16),
            pltpu.SemaphoreType.DMA((2,)),
            pltpu.SemaphoreType.DMA((3 + ITERS,)),
            pltpu.SemaphoreType.DMA((3 + ITERS,)),
            pltpu.SemaphoreType.DMA((2 * ITERS, 8)),
            pltpu.SemaphoreType.DMA((2 * ITERS, 8)),
            pltpu.SemaphoreType.DMA((ITERS, 2)),
            pltpu.SemaphoreType.DMA((ITERS, 2)),
        ],
        compiler_params=pltpu.CompilerParams(
            collective_id=0, has_side_effects=True, vmem_limit_bytes=48 * 1024 * 1024
        ),
        name="fista",
    )(
        observed.reshape(per, 2, 8, cols),
        history.reshape(hist, 2, 8, 128),
        spikes_start.reshape(per, 2, 8, cols),
        kernel.reshape(1, -1),
        smooth_half,
    )
    shape = spikes_start.shape
    return spikes.reshape(shape), point.reshape(shape)


def solution(mesh):
    in_specs = (
        P("frames", None, "rows", None),
        P(None, None, "rows", "frames"),
        P("frames", None, "rows", None),
        P(),
        P(),
    )
    out_specs = (P("frames", None, "rows", None), P("frames", None, "rows", None))
    step = functools.partial(shards, mesh.shape["frames"], mesh.shape["rows"])
    return jax.shard_map(step, mesh=mesh, in_specs=in_specs, out_specs=out_specs, check_vma=False)
```

profile of v0, /device:TPU:1, one launch (start us, length us, event | category | flops | bytes accessed | tf_op | source)
XLA Modules:
  0.0 87.1 jit_solution(15751009934214644124)
XLA Ops:
  0.6 0.0 copy-start.3
  0.6 0.0 copy-start.4
  0.7 0.6 copy-done.3
  1.3 0.0 copy-done.4
  1.3 0.0 copy-start
  1.3 1.0 %copy-done = f32[4,1,16,2048]{3,2,1,0:T(8,128)S(1)} copy-done((f32[4,1,16,2048]{3,2,1,0:T(8,128)S(1)}, f32[4,1,16,2048]{3,2,1,0:T(8,128)}, u32[]{:S(2)}) %copy-start) | copy-done | bytes 524312
  2.3 0.0 copy-start.1
  2.3 1.0 %copy-done.1 = bf16[127,1,16,128]{3,2,1,0:T(8,128)(2,1)S(1)} copy-done((bf16[127,1,16,128]{3,2,1,0:T(8,128)(2,1)S(1)}, bf16[127,1,16,128]{3,2,1,0:T(8,128)(2,1)}, u32[]{:S(2)}) %copy-start.1) | copy-done | bytes 520216
  3.4 0.0 copy-start.2
  3.4 0.9 %copy-done.2 = bf16[4,1,16,2048]{3,2,1,0:T(8,128)(2,1)S(1)} copy-done((bf16[4,1,16,2048]{3,2,1,0:T(8,128)(2,1)S(1)}, bf16[4,1,16,2048]{3,2,1,0:T(8,128)(2,1)}, u32[]{:S(2)}) %copy-start.2) | copy-done | bytes 262168
  4.3 81.2 %fista.1 = (f32[4,2,8,2048]{3,2,1,0:T(8,128)S(1)}, f32[4,2,8,2048]{3,2,1,0:T(8,128)S(1)}) custom-call(bf16[4,2,8,2048]{3,2,1,0:T(8,128)(2,1)S(1)} %bitcast.14, bf16[127,2,8,128]{3,2,1,0:T(8,128)(2,1)S(1)} %bitcast.13, f32[4,2,8,2048]{3,2,1,0:T(8,128)S(1)} %bitcast.10, bf16[1,128]{1,0:T(2,128)(2,1)S(1)} %bitcast.15, f32[8]{0:T(128)S(1)} %copy-done.4), custom_call_target="tpu_custom_call" | custom-call | tf_op jit(solution)/shard_map/fista/pallas_call | solution.py:475
  85.5 0.8 copy.11
  86.3 0.8 copy.12
Async XLA Ops:
  0.6 0.7 copy-start.3
  0.6 0.7 copy-start.4
  1.3 1.0 %copy-start = (f32[4,1,16,2048]{3,2,1,0:T(8,128)S(1)}, f32[4,1,16,2048]{3,2,1,0:T(8,128)}, u32[]{:S(2)}) copy-start(f32[4,1,16,2048]{3,2,1,0:T(8,128)} %param.7) | copy-start | bytes 1572868
  2.3 1.0 %copy-start.1 = (bf16[127,1,16,128]{3,2,1,0:T(8,128)(2,1)S(1)}, bf16[127,1,16,128]{3,2,1,0:T(8,128)(2,1)}, u32[]{:S(2)}) copy-start(bf16[127,1,16,128]{3,2,1,0:T(8,128)(2,1)} %param.6) | copy-start | bytes 1560580
  3.4 0.9 %copy-start.2 = (bf16[4,1,16,2048]{3,2,1,0:T(8,128)(2,1)S(1)}, bf16[4,1,16,2048]{3,2,1,0:T(8,128)(2,1)}, u32[]{:S(2)}) copy-start(bf16[4,1,16,2048]{3,2,1,0:T(8,128)(2,1)} %param.5) | copy-start | bytes 786436
where the time goes:
time: 87.3 us; the launch traced here: 87.1 us
  Pallas kernels  81.2 us (93%)
  local copies, waits for them, and re-layouts  5.27 us (6%)
    pallas_call x1, Pallas kernels, shards(): pl.pallas_call(functools.partial(body, nf, nr, frames), out_shape=(out, o...  81.2 us
    unnamed x12, local copies, waits for them, and re-layouts  5.27 us

commit v1 on v0

--- a/solution.py
+++ b/solution.py
@@ -51,10 +51,11 @@
     obs_hbm,
     hist_hbm,
     start_hbm,
-    taps_ref,
-    half_ref,
-    out_spikes,
-    out_point,
+    taps_hbm,
+    half_hbm,
+    out_first,
+    out_slope,
+    out_step,
     start_f,
     hi_f,
     lo_f,
@@ -62,8 +63,17 @@
     lo_c,
     obs_c,
     hist_v,
-    grad_c,
-    grad_f,
+    back_c,
+    back_f,
+    point_1,
+    above_f,
+    below_f,
+    pull_f,
+    first_f,
+    slope_f,
+    store_sems,
+    taps_ref,
+    half_ref,
     edge_s,
     strip_s,
     above,
@@ -87,6 +97,8 @@
     halo_recv,
     sum_send,
     sum_recv,
+    wide_send,
+    wide_recv,
 ):
     col = lax.axis_index("frames")
     row = lax.axis_index("rows")
@@ -99,11 +111,10 @@
     load_start.start()
     load_hist = pltpu.make_async_copy(hist_hbm, hist_v.at[pl.ds(0, hist_len)], local_sems.at[1])
     load_hist.start()
-
-    above[...] = jnp.zeros(above.shape, BF16)
-    below[...] = jnp.zeros(below.shape, BF16)
-    strips[...] = jnp.zeros(strips.shape, BF16)
-    hist_v[hist_len:] = jnp.zeros((hist_v.shape[0] - hist_len,) + hist_v.shape[1:], BF16)
+    load_taps = pltpu.make_async_copy(taps_hbm, taps_ref, local_sems.at[2])
+    load_taps.start()
+    load_half = pltpu.make_async_copy(half_hbm, half_ref, local_sems.at[3])
+    load_half.start()
 
     barrier = pltpu.get_barrier_semaphore()
 
@@ -187,19 +198,89 @@
 
     to_block(0, lambda c: hi_f.at[c], hi_c)
     to_block(1, lambda c: obs_hbm.at[:, :, :, pl.ds(pl.multiple_of(c * 128, 128), 128)], obs_c)
-    to_block(2, lambda c: lo_f.at[c], lo_c)
-
-    def gradient_out(it):
-        target = grad_f.at[it, col]
+
+    def back_out(it):
+        target = back_f.at[it, col]
         exchange(
             3 + it,
-            lambda f: grad_c.at[it, pl.ds(f * per, per)],
+            lambda f: back_c.at[it, pl.ds(f * per, per)],
             target,
-            grad_c.at[it, pl.ds(col * per, per)],
+            back_c.at[it, pl.ds(col * per, per)],
             target,
         )
 
+    def wide_copies(it, buffer):
+        copies = [((0, -1), 0, below_f), ((0, 1), 1, above_f)]
+        return [
+            (
+                where,
+                pltpu.make_async_remote_copy(
+                    src_ref=buffer.at[:, :, h],
+                    dst_ref=target.at[it],
+                    send_sem=wide_send.at[it, h],
+                    recv_sem=wide_recv.at[it, h],
+                    device_id={"rows": row + where[1]},
+                    device_id_type=MESH,
+                ),
+            )
+            for where, h, target in copies
+        ]
+
+    def start_all(copies):
+        for where, copy in copies:
+
+            @pl.when(exists[where])
+            def _():
+                copy.start()
+
+    def recv_all(copies):
+        for where, copy in copies:
+
+            @pl.when(exists[-where[0], -where[1]])
+            def _():
+                copy.wait_recv()
+
+    def send_all(copies):
+        for where, copy in copies:
+
+            @pl.when(exists[where])
+            def _():
+                copy.wait_send()
+
+    start_all(wide_copies(0, hi_f))
+
+    def clear(ref):
+        ref[...] = jnp.zeros(ref.shape, BF16)
+
+    @pl.when(row == 0)
+    def _():
+        clear(above)
+        clear(above_f)
+        clear(strips.at[:, 0])
+
+    @pl.when(row == nr - 1)
+    def _():
+        clear(below)
+        clear(below_f)
+        clear(strips.at[:, 2])
+
+    @pl.when(col == 0)
+    def _():
+        clear(strips.at[:, :, :, pl.ds(0, 128)])
+
+    @pl.when(col == nf - 1)
+    def _():
+        clear(strips.at[:, :, :, pl.ds(128, 128)])
+
+    for n in range(1, 2 * ITERS, 2):
+        clear(above.at[n, pl.ds(rows // 2, rows // 2)])
+        clear(below.at[n, pl.ds(0, rows // 2)])
+
+    hist_v[hist_len:] = jnp.zeros((hist_v.shape[0] - hist_len,) + hist_v.shape[1:], BF16)
+
     size = 256
+    load_taps.wait()
+    load_half.wait()
     spread = jnp.concatenate(
         [taps_ref[...].astype(F32), jnp.zeros((1, size - tap_count), F32)], axis=1
     )
@@ -238,7 +319,7 @@
             value = jnp.where(distance == k, half[k], value)
         return value
 
-    high, low = split(taps_at(jnp.abs(iota((128, 128), 0) - iota((128, 128), 1))))
+    high, low = split(taps_at(jnp.abs(iota((384, 128), 0) - 128 - iota((384, 128), 1))))
     band[:, 0:128] = high
     band[:, 128:256] = low
 
@@ -275,10 +356,15 @@
 
     chunk = rows // GROUPS
 
+    def edge_rows(n):
+        cut = rows // 2 if n % 2 else rows
+        return pl.ds(0, cut), pl.ds(rows - cut, cut)
+
     def halo_copies(n):
+        upper, lower = edge_rows(n)
         copies = [
-            ((0, -1), edge_s.at[n, 0], below.at[n], 1),
-            ((0, 1), edge_s.at[n, 1], above.at[n], 0),
+            ((0, -1), edge_s.at[n, 0, lower], below.at[n, lower], 1),
+            ((0, 1), edge_s.at[n, 1, upper], above.at[n, upper], 0),
         ]
         for dc in (-1, 1):
             side = 0 if dc == 1 else 1
@@ -307,30 +393,21 @@
         ]
 
     def halo_start(n, field):
-        edge_s[n, 0] = field[:, 0:128]
-        edge_s[n, 1] = field[:, 128:256]
+        upper, lower = edge_rows(n)
+        weight = jnp.asarray(2.0 if n % 2 else 1.0, BF16)
+        edge_s[n, 0, lower] = field[rows - lower.size :, 0:128] * weight
+        edge_s[n, 1, upper] = field[: upper.size, 128:256] * weight
         wide = [field[g * chunk : (g + 1) * chunk, :] for g in range(GROUPS)]
         packed = dot(jnp.concatenate(wide, axis=1), sel[...]).astype(BF16)
         strip_s[n, 0] = packed[:, 0:128]
         strip_s[n, 1] = packed[:, 128:256]
-        for where, copy in halo_copies(n):
-
-            @pl.when(exists[where])
-            def _():
-                copy.start()
-
-    def halo_wait(n):
-        for where, copy in halo_copies(n):
-
-            @pl.when(exists[-where[0], -where[1]])
-            def _():
-                copy.wait_recv()
+        start_all(halo_copies(n))
 
     def smooth(n, field):
         stacked = jnp.concatenate(
             [above[n], field[:, 0:128], field[:, 128:256], below[n]], axis=0
         )
-        wide = dot(stacked, band[...])
+        wide = dot(stacked, band[128:256])
         flat = wide[:, 0:128] + wide[:, 128:256]
         lines = strips[n].reshape(3 * chunk, 256)
         corner = dot(lines, hbh[...]) + dot(lines, hbl[...])
@@ -340,9 +417,40 @@
                 corner[which * chunk : (which + 1) * chunk, g * 256 + h * 128 : g * 256 + h * 128 + 128]
                 for g in range(GROUPS)
             ]
+            if n % 2 and which != 1:
+                gone = jnp.zeros((chunk, 128), F32)
+                kept = (0, 1, 2, 3) if which == 0 else (4, 5, 6, 7)
+                extra = [2.0 * extra[g] if g in kept else gone for g in range(GROUPS)]
             return flat[block * rows : (block + 1) * rows] + jnp.concatenate(extra, axis=0)
 
-        blocks = [part(0, 0, 1), part(1, 1, 0), part(2, 1, 1), part(3, 2, 0)]
+        return along_rows([part(0, 0, 1), part(1, 1, 0), part(2, 1, 1), part(3, 2, 0)])
+
+    def smooth_wide(it, buffer):
+        blocks = [above_f[it], buffer[:, :, 0], buffer[:, :, 1], below_f[it]]
+        blocks = [b.astype(F32).reshape(rows, 128).astype(BF16) for b in blocks]
+        step = 8 * per
+        gap = jnp.zeros((step, 128), BF16)
+        stacked = jnp.concatenate(
+            [
+                jnp.concatenate(
+                    [
+                        jnp.concatenate([gap, b[: rows - step]], axis=0),
+                        b,
+                        jnp.concatenate([b[step:], gap], axis=0),
+                    ],
+                    axis=1,
+                )
+                for b in blocks
+            ],
+            axis=0,
+        )
+        wide = dot(stacked, band[...])
+        flat = wide[:, 0:128] + wide[:, 128:256]
+        field = jnp.concatenate(blocks[1:3], axis=1).astype(F32)
+        blocks = [flat[b * rows : (b + 1) * rows] for b in range(4)]
+        pull_f[it] = REG_WEIGHT * (field - along_rows(blocks))
+
+    def along_rows(blocks):
         pairs = [split(b) for b in blocks]
         result = []
         for q in range(rows // rg):
@@ -363,7 +471,8 @@
 
     lane = iota((1, 128), 1)
 
-    def reduce_over(it, stage, axis, count, me, value):
+    def sum_start(it, stage, value):
+        axis, me, count = (("rows", row, nr), ("frames", col, nf))[stage]
         row_s[it, stage] = value
         row_r[it, stage, pl.ds(me, 1)] = value.reshape(1, 1, 128)
 
@@ -379,45 +488,97 @@
             return carry
 
         lax.fori_loop(1, count, send, 0)
+
+    def sum_end(it, stage):
+        count = (nr, nf)[stage]
         wait_bytes(row_r.at[it, stage, pl.ds(0, count - 1)], sum_recv.at[it, stage])
         return jnp.sum(row_r[it, stage], axis=0)
 
-    def step_size(it, norm, conv, curv):
-        value = jnp.where(lane == 0, norm, jnp.where(lane == 1, conv, curv))
-        value = reduce_over(it, 0, "frames", nf, col, value)
-        value = reduce_over(it, 1, "rows", nr, row, value)
-        return value[:, 0:1] / (value[:, 1:2] + REG_WEIGHT * value[:, 2:3])
-
     def total_of(value):
         return jnp.sum(value, keepdims=True)
 
+    recv_all(wide_copies(0, hi_f))
+    smooth_wide(0, hi_f)
+
+    def descend(point, pull, back, step):
+        return jnp.maximum(point - step * (back + pull) - step * SPARSE_WEIGHT, 0.0)
+
+    def wide_parts(c, h):
+        cut = slice(c * 8 * per, (c + 1) * 8 * per)
+        return cut, slice(h * 128, (h + 1) * 128)
+
+    def update_first(step):
+        wait_bytes(back_f.at[0], a2a_recv.at[3])
+        for c in range(nf):
+            for h in (0, 1):
+                cut, lanes = wide_parts(c, h)
+                where = slice(c * 128, (c + 1) * 128)
+                point = start_f[:, h, :, where].reshape(8 * per, 128)
+                back = back_f[0, c, :, h].astype(F32).reshape(8 * per, 128)
+                updated = descend(point, pull_f[0, cut, lanes], back, step).reshape(per, 8, 128)
+                first_f[:, h, :, where] = updated
+                point_1[c, :, h] = updated.astype(BF16)
+        start_all(wide_copies(1, point_1))
+        store = pltpu.make_async_copy(first_f, out_first, store_sems.at[0])
+        store.start()
+        return store
+
+    def slope_last():
+        wait_bytes(back_f.at[1], a2a_recv.at[4])
+        for c in range(nf):
+            for h in (0, 1):
+                cut, lanes = wide_parts(c, h)
+                back = back_f[1, c, :, h].astype(F32).reshape(8 * per, 128)
+                slope = (back + pull_f[1, cut, lanes]).reshape(per, 8, 128)
+                slope_f[:, h, :, c * 128 : (c + 1) * 128] = slope
+        store = pltpu.make_async_copy(slope_f, out_slope, store_sems.at[1])
+        store.start()
+        return store
+
+    steps = []
     wait_bytes(hi_c, a2a_recv.at[0])
     point_bf = halves(hi_c).astype(BF16)
     halo_start(0, point_bf)
-    seen = None
-    steps = []
     for it in range(ITERS):
         now = dot(kw[...], point_bf)
         if it == 0:
             wait_bytes(obs_c, a2a_recv.at[1])
             past = past - halves(obs_c)
         resid_bf = (past + now).astype(BF16)
-        back = dot(kwt[...], resid_bf).astype(BF16).astype(F32)
-        halo_wait(2 * it)
+        back = dot(kwt[...], resid_bf)
+        for h in (0, 1):
+            part = back[:, h * 128 : (h + 1) * 128].reshape(frames, 8, 128)
+            back_c[it, :, h] = part.astype(BF16)
+        back = back.astype(BF16).astype(F32)
+        recv_all(halo_copies(2 * it))
         point_f = point_bf.astype(F32)
         gradient = back + REG_WEIGHT * (point_f - smooth(2 * it, point_bf))
-        for h in (0, 1):
-            grad_c[it, :, h] = gradient[:, h * 128 : (h + 1) * 128].reshape(frames, 8, 128)
         grad_bf = gradient.astype(BF16)
         halo_start(2 * it + 1, grad_bf)
-        gradient_out(it)
+        if it == 0:
+            to_block(2, lambda c: lo_f.at[c], lo_c)
+        else:
+            back_out(1)
         conv = dot(kw[...], grad_bf)
         norm, conv = total_of(gradient * gradient), total_of(conv * conv)
-        halo_wait(2 * it + 1)
+        if it == 1:
+            store_first = update_first(steps[0])
+        recv_all(halo_copies(2 * it + 1))
         grad_smooth = smooth(2 * it + 1, grad_bf)
         grad_f32 = grad_bf.astype(F32)
         curv = total_of(grad_f32 * (grad_f32 - grad_smooth))
-        step = step_size(it, norm, conv, curv)
+        sum_start(it, 0, jnp.where(lane == 0, norm, jnp.where(lane == 1, conv, curv)))
+        if it == 1:
+            recv_all(wide_copies(1, point_1))
+            smooth_wide(1, point_1)
+        value = sum_end(it, 0)
+        sum_start(it, 1, value)
+        if it == 0:
+            back_out(0)
+        else:
+            store_slope = slope_last()
+        value = sum_end(it, 1)
+        step = value[:, 0:1] / (value[:, 1:2] + REG_WEIGHT * value[:, 2:3])
         steps.append(step)
         if it == 0:
             wait_bytes(lo_c, a2a_recv.at[2])
@@ -425,37 +586,20 @@
             point = jnp.maximum(point - step * gradient - step * SPARSE_WEIGHT, 0.0)
             point_bf = point.astype(BF16)
             halo_start(2, point_bf)
-
-    betas = momentum_terms(ITERS)
-    for it in range(ITERS):
-        wait_bytes(grad_f.at[it], a2a_recv.at[3 + it])
-    for c in range(nf):
-        cut = slice(c * 128, (c + 1) * 128)
-        previous = start_f[:, :, :, cut]
-        point = previous
-        for it in range(ITERS):
-            step = steps[it].reshape(1, 1, 1, 1)
-            updated = jnp.maximum(
-                point - step * grad_f[it, c] - step * SPARSE_WEIGHT, 0.0
-            )
-            point = updated + betas[it] * (updated - previous) if betas[it] else updated
-            previous = updated
-        out_spikes[:, :, :, cut] = previous
-        out_point[:, :, :, cut] = point
+    out_step[...] = jnp.broadcast_to(step, out_step.shape)
+    store_first.wait()
+    store_slope.wait()
 
     wait_bytes(hi_f.at[pl.ds(0, nf - 1)], a2a_send.at[0])
     wait_bytes(obs_c.at[pl.ds(0, per * (nf - 1))], a2a_send.at[1])
     wait_bytes(lo_f.at[pl.ds(0, nf - 1)], a2a_send.at[2])
     for it in range(ITERS):
-        wait_bytes(grad_f.at[it, pl.ds(0, nf - 1)], a2a_send.at[3 + it])
-        for stage, count in ((0, nf), (1, nr)):
+        wait_bytes(back_f.at[it, pl.ds(0, nf - 1)], a2a_send.at[3 + it])
+        for stage, count in ((0, nr), (1, nf)):
             wait_bytes(row_r.at[it, stage, pl.ds(0, count - 1)], sum_send.at[it, stage])
+        send_all(wide_copies(it, hi_f if it == 0 else point_1))
         for n in (2 * it, 2 * it + 1):
-            for where, copy in halo_copies(n):
-
-                @pl.when(exists[where])
-                def _():
-                    copy.wait_send()
+            send_all(halo_copies(n))
 
 
 def shards(nf, nr, observed, history, spikes_start, kernel, smooth_half):
@@ -469,14 +613,14 @@
     chunk = rows // GROUPS
     most = max(nf, nr)
     block = (per, 2, 8, 128)
-    any_spec = pl.BlockSpec(memory_space=pl.ANY)
+    any_spec = pl.BlockSpec(memory_space=pltpu.MemorySpace.HBM)
     vmem = pl.BlockSpec(memory_space=pltpu.VMEM)
     out = jax.ShapeDtypeStruct((per, 2, 8, cols), F32)
-    spikes, point = pl.pallas_call(
+    first, slope, step = pl.pallas_call(
         functools.partial(body, nf, nr, frames),
-        out_shape=(out, out),
-        in_specs=[any_spec, any_spec, any_spec, vmem, pl.BlockSpec(memory_space=pltpu.SMEM)],
-        out_specs=(vmem, vmem),
+        out_shape=(out, out, jax.ShapeDtypeStruct((1, 128), F32)),
+        in_specs=[any_spec] * 5,
+        out_specs=(any_spec, any_spec, vmem),
         scratch_shapes=[
             pltpu.VMEM((per, 2, 8, cols), F32),
             pltpu.VMEM((nf,) + block, BF16),
@@ -485,8 +629,17 @@
             pltpu.VMEM((frames, 2, 8, 128), BF16),
             pltpu.VMEM((frames, 2, 8, 128), BF16),
             pltpu.VMEM((hist_pad, 2, 8, 128), BF16),
-            pltpu.VMEM((ITERS, frames, 2, 8, 128), F32),
-            pltpu.VMEM((ITERS, nf) + block, F32),
+            pltpu.VMEM((ITERS, frames, 2, 8, 128), BF16),
+            pltpu.VMEM((ITERS, nf) + block, BF16),
+            pltpu.VMEM((nf,) + block, BF16),
+            pltpu.VMEM((ITERS, nf, per, 8, 128), BF16),
+            pltpu.VMEM((ITERS, nf, per, 8, 128), BF16),
+            pltpu.VMEM((ITERS, rows, 256), F32),
+            pltpu.VMEM((per, 2, 8, cols), F32),
+            pltpu.VMEM((per, 2, 8, cols), F32),
+            pltpu.SemaphoreType.DMA((2,)),
+            pltpu.VMEM((1, kernel.shape[0]), BF16),
+            pltpu.SMEM(smooth_half.shape, F32),
             pltpu.VMEM((2 * ITERS, 2, rows, 128), BF16),
             pltpu.VMEM((2 * ITERS, 2, chunk, 128), BF16),
             pltpu.VMEM((2 * ITERS, rows, 128), BF16),
@@ -497,22 +650,24 @@
             pltpu.VMEM((rows, 8 * hist_pad), BF16),
             pltpu.VMEM((rows, rows), BF16),
             pltpu.VMEM((rows, rows), BF16),
-            pltpu.VMEM((128, 256), BF16),
+            pltpu.VMEM((384, 256), BF16),
             pltpu.VMEM((rg, 3 * rg), BF16),
             pltpu.VMEM((rg, 3 * rg), BF16),
             pltpu.VMEM((GROUPS * 256, 256), BF16),
             pltpu.VMEM((256, GROUPS * 256), BF16),
             pltpu.VMEM((256, GROUPS * 256), BF16),
-            pltpu.SemaphoreType.DMA((2,)),
+            pltpu.SemaphoreType.DMA((4,)),
             pltpu.SemaphoreType.DMA((3 + ITERS,)),
             pltpu.SemaphoreType.DMA((3 + ITERS,)),
             pltpu.SemaphoreType.DMA((2 * ITERS, 8)),
             pltpu.SemaphoreType.DMA((2 * ITERS, 8)),
             pltpu.SemaphoreType.DMA((ITERS, 2)),
             pltpu.SemaphoreType.DMA((ITERS, 2)),
+            pltpu.SemaphoreType.DMA((ITERS, 2)),
+            pltpu.SemaphoreType.DMA((ITERS, 2)),
         ],
         compiler_params=pltpu.CompilerParams(
-            collective_id=0, has_side_effects=True, vmem_limit_bytes=48 * 1024 * 1024
+            collective_id=0, has_side_effects=True, vmem_limit_bytes=67043328
         ),
         name="fista",
     )(
@@ -523,7 +678,11 @@
         smooth_half,
     )
     shape = spikes_start.shape
-    return spikes.reshape(shape), point.reshape(shape)
+    step = step[0, 0]
+    beta = momentum_terms(ITERS)[-1]
+    first, slope = first.reshape(shape), slope.reshape(shape)
+    spikes = jnp.maximum(first - step * slope - step * SPARSE_WEIGHT, 0.0)
+    return spikes, spikes + beta * (spikes - first)
 
 
 def solution(mesh):

time: 87.3 us -> 76.4 us (0.88)
  Pallas kernels: 81.2 us -> 72.6 us
  local copies, waits for them, and re-layouts: 5.27 us -> 0.66 us
  other arithmetic: 0 us -> 2.35 us
    pallas_call x1, Pallas kernels: 81.2 us -> 72.6 us  [shards(): pl.pallas_call(functools.partial(body, nf, nr, frames), out_shape=(out, o...]
    unnamed x12 -> x2, local copies, waits for them, and re-layouts: 5.27 us -> 0.66 us
    add x0 -> x1, other arithmetic: none -> 2.35 us  [shards(): return (spikes, spikes + beta * (spikes - first))]
where the time goes in v1:
time: 76.4 us; the launch traced here: 76.3 us
  Pallas kernels  72.6 us (95%)
  other arithmetic  2.35 us (3%)
    pallas_call x1, Pallas kernels, shards(): pl.pallas_call(functools.partial(body, nf, nr, frames), out_shape=(out, o...  72.6 us
    add x1, other arithmetic, shards(): return (spikes, spikes + beta * (spikes - first))  2.35 us

profile of v1, /device:TPU:1, one launch (start us, length us, event | category | flops | bytes accessed | tf_op | source)
XLA Modules:
  0.0 76.3 jit_solution(7435519777889694079)
XLA Ops:
  0.6 72.6 %fista.1 = (f32[4,2,8,2048]{3,2,1,0:T(8,128)}, f32[4,2,8,2048]{3,2,1,0:T(8,128)}, f32[1,128]{1,0:T(1,128)}) custom-call(bf16[4,2,8,2048]{3,2,1,0:T(8,128)(2,1)} %bitcast.27, bf16[127,2,8,128]{3,2,1,0:T(8,128)(2,1)} %bitcast.26, f32[4,2,8,2048]{3,2,1,0:T(8,128)} %bitcast.25, bf16[1,128]{1,0:T(2,128)(2,1)} %bitcast.28, f32[8]{0:T(128)} %half_hbm.1), custom_call_target="tpu_custom_call" | custom-call | tf_op jit(solution)/shard_map/fista/pallas_call | solution.py:619
  73.2 0.0 copy-start
  73.2 0.7 copy-done
  73.9 2.4 %fusion.3 = (f32[4,1,16,2048]{3,2,1,0:T(8,128)}, f32[4,1,16,2048]{3,2,1,0:T(8,128)}) fusion(f32[4,2,8,2048]{3,2,1,0:T(8,128)} %get-tuple-element.5, f32[]{:T(128)S(6)} %mul.41, f32[4,2,8,2048]{3,2,1,0:T(8,128)} %get-tuple-element.7, f32[]{:T(128)S(1)} %bitcast.30), kind=kLoop, calls=%fused_computation.5 | loop fusion | flops 917504 | bytes 2097160 | tf_op jit(solution)/shard_map/add | solution.py:685
Async XLA Ops:
  73.2 0.7 copy-start

commit v2 on v1

--- a/solution.py
+++ b/solution.py
@@ -15,6 +15,8 @@
 F32 = jnp.float32
 BF16 = jnp.bfloat16
 GROUPS = 8
+HALOS = 6
+CURVATURE = (1, 3)
 
 
 def momentum_terms(count):
@@ -272,10 +274,6 @@
     def _():
         clear(strips.at[:, :, :, pl.ds(128, 128)])
 
-    for n in range(1, 2 * ITERS, 2):
-        clear(above.at[n, pl.ds(rows // 2, rows // 2)])
-        clear(below.at[n, pl.ds(0, rows // 2)])
-
     hist_v[hist_len:] = jnp.zeros((hist_v.shape[0] - hist_len,) + hist_v.shape[1:], BF16)
 
     size = 256
@@ -357,15 +355,34 @@
     chunk = rows // GROUPS
 
     def edge_rows(n):
-        cut = rows // 2 if n % 2 else rows
+        cut = rows // 2 if n in CURVATURE else rows
         return pl.ds(0, cut), pl.ds(rows - cut, cut)
+
+    def edge_copy(n, dr, part, slot):
+        source, target = (edge_s.at[n, 0], below) if dr == -1 else (edge_s.at[n, 1], above)
+        return (
+            (0, dr),
+            pltpu.make_async_remote_copy(
+                src_ref=source.at[part],
+                dst_ref=target.at[n, part],
+                send_sem=halo_send.at[n, slot],
+                recv_sem=halo_recv.at[n, slot],
+                device_id={"rows": row + dr},
+                device_id_type=MESH,
+            ),
+        )
+
+    def rest_copies(n):
+        half_rows = rows // 2
+        return [
+            edge_copy(n, -1, pl.ds(0, half_rows), 8),
+            edge_copy(n, 1, pl.ds(half_rows, half_rows), 9),
+        ]
 
     def halo_copies(n):
         upper, lower = edge_rows(n)
-        copies = [
-            ((0, -1), edge_s.at[n, 0, lower], below.at[n, lower], 1),
-            ((0, 1), edge_s.at[n, 1, upper], above.at[n, upper], 0),
-        ]
+        result = [edge_copy(n, -1, lower, 1), edge_copy(n, 1, upper, 0)]
+        copies = []
         for dc in (-1, 1):
             side = 0 if dc == 1 else 1
             for dr in (-1, 0, 1):
@@ -377,7 +394,7 @@
                         2 + side * 3 + 1 - dr,
                     )
                 )
-        return [
+        return result + [
             (
                 where,
                 pltpu.make_async_remote_copy(
@@ -393,10 +410,8 @@
         ]
 
     def halo_start(n, field):
-        upper, lower = edge_rows(n)
-        weight = jnp.asarray(2.0 if n % 2 else 1.0, BF16)
-        edge_s[n, 0, lower] = field[rows - lower.size :, 0:128] * weight
-        edge_s[n, 1, upper] = field[: upper.size, 128:256] * weight
+        edge_s[n, 0] = field[:, 0:128]
+        edge_s[n, 1] = field[:, 128:256]
         wide = [field[g * chunk : (g + 1) * chunk, :] for g in range(GROUPS)]
         packed = dot(jnp.concatenate(wide, axis=1), sel[...]).astype(BF16)
         strip_s[n, 0] = packed[:, 0:128]
@@ -404,8 +419,14 @@
         start_all(halo_copies(n))
 
     def smooth(n, field):
+        if n in CURVATURE:
+            cut = rows // 2
+            gone, twice = jnp.zeros((cut, 128), BF16), jnp.asarray(2.0, BF16)
+            outer = [above[n, 0:cut] * twice, gone], [gone, below[n, cut:rows] * twice]
+        else:
+            outer = [above[n]], [below[n]]
         stacked = jnp.concatenate(
-            [above[n], field[:, 0:128], field[:, 128:256], below[n]], axis=0
+            [*outer[0], field[:, 0:128], field[:, 128:256], *outer[1]], axis=0
         )
         wide = dot(stacked, band[128:256])
         flat = wide[:, 0:128] + wide[:, 128:256]
@@ -417,7 +438,7 @@
                 corner[which * chunk : (which + 1) * chunk, g * 256 + h * 128 : g * 256 + h * 128 + 128]
                 for g in range(GROUPS)
             ]
-            if n % 2 and which != 1:
+            if n in CURVATURE and which != 1:
                 gone = jnp.zeros((chunk, 128), F32)
                 kept = (0, 1, 2, 3) if which == 0 else (4, 5, 6, 7)
                 extra = [2.0 * extra[g] if g in kept else gone for g in range(GROUPS)]
@@ -539,6 +560,7 @@
     wait_bytes(hi_c, a2a_recv.at[0])
     point_bf = halves(hi_c).astype(BF16)
     halo_start(0, point_bf)
+    to_block(2, lambda c: lo_f.at[c], lo_c)
     for it in range(ITERS):
         now = dot(kw[...], point_bf)
         if it == 0:
@@ -550,15 +572,16 @@
             part = back[:, h * 128 : (h + 1) * 128].reshape(frames, 8, 128)
             back_c[it, :, h] = part.astype(BF16)
         back = back.astype(BF16).astype(F32)
-        recv_all(halo_copies(2 * it))
+        if it == 0:
+            recv_all(halo_copies(0))
         point_f = point_bf.astype(F32)
         gradient = back + REG_WEIGHT * (point_f - smooth(2 * it, point_bf))
         grad_bf = gradient.astype(BF16)
         halo_start(2 * it + 1, grad_bf)
+        back_out(it)
         if it == 0:
-            to_block(2, lambda c: lo_f.at[c], lo_c)
-        else:
-            back_out(1)
+            start_all(rest_copies(1))
+            halo_start(4, (gradient - grad_bf.astype(F32)).astype(BF16))
         conv = dot(kw[...], grad_bf)
         norm, conv = total_of(gradient * gradient), total_of(conv * conv)
         if it == 1:
@@ -568,24 +591,33 @@
         grad_f32 = grad_bf.astype(F32)
         curv = total_of(grad_f32 * (grad_f32 - grad_smooth))
         sum_start(it, 0, jnp.where(lane == 0, norm, jnp.where(lane == 1, conv, curv)))
-        if it == 1:
+        if it == 0:
+            wait_bytes(lo_c, a2a_recv.at[2])
+            low = halves(lo_c)
+            halo_start(5, low.astype(BF16))
+        else:
             recv_all(wide_copies(1, point_1))
             smooth_wide(1, point_1)
         value = sum_end(it, 0)
         sum_start(it, 1, value)
         if it == 0:
-            back_out(0)
+            recv_all(rest_copies(1))
+            recv_all(halo_copies(4))
+            recv_all(halo_copies(5))
         else:
             store_slope = slope_last()
         value = sum_end(it, 1)
         step = value[:, 0:1] / (value[:, 1:2] + REG_WEIGHT * value[:, 2:3])
         steps.append(step)
         if it == 0:
-            wait_bytes(lo_c, a2a_recv.at[2])
-            point = halves(hi_c) + halves(lo_c)
-            point = jnp.maximum(point - step * gradient - step * SPARSE_WEIGHT, 0.0)
+            point = descend(halves(hi_c) + low, 0.0, gradient, step)
             point_bf = point.astype(BF16)
-            halo_start(2, point_bf)
+            for ref in (above, below, strips):
+                start, slope = (
+                    ref[high].astype(F32) + ref[low_part].astype(F32)
+                    for high, low_part in ((0, 5), (1, 4))
+                )
+                ref[2] = descend(start, 0.0, slope, step).astype(BF16)
     out_step[...] = jnp.broadcast_to(step, out_step.shape)
     store_first.wait()
     store_slope.wait()
@@ -598,8 +630,9 @@
         for stage, count in ((0, nr), (1, nf)):
             wait_bytes(row_r.at[it, stage, pl.ds(0, count - 1)], sum_send.at[it, stage])
         send_all(wide_copies(it, hi_f if it == 0 else point_1))
-        for n in (2 * it, 2 * it + 1):
+        for n in ((0, 1, 3), (4, 5))[it]:
             send_all(halo_copies(n))
+    send_all(rest_copies(1))
 
 
 def shards(nf, nr, observed, history, spikes_start, kernel, smooth_half):
@@ -640,11 +673,11 @@
             pltpu.SemaphoreType.DMA((2,)),
             pltpu.VMEM((1, kernel.shape[0]), BF16),
             pltpu.SMEM(smooth_half.shape, F32),
-            pltpu.VMEM((2 * ITERS, 2, rows, 128), BF16),
-            pltpu.VMEM((2 * ITERS, 2, chunk, 128), BF16),
-            pltpu.VMEM((2 * ITERS, rows, 128), BF16),
-            pltpu.VMEM((2 * ITERS, rows, 128), BF16),
-            pltpu.VMEM((2 * ITERS, 3, chunk, 256), BF16),
+            pltpu.VMEM((HALOS, 2, rows, 128), BF16),
+            pltpu.VMEM((HALOS, 2, chunk, 128), BF16),
+            pltpu.VMEM((HALOS, rows, 128), BF16),
+            pltpu.VMEM((HALOS, rows, 128), BF16),
+            pltpu.VMEM((HALOS, 3, chunk, 256), BF16),
             pltpu.VMEM((ITERS, 2, 1, 128), F32),
             pltpu.VMEM((ITERS, 2, most, 1, 128), F32),
             pltpu.VMEM((rows, 8 * hist_pad), BF16),
@@ -659,8 +692,8 @@
             pltpu.SemaphoreType.DMA((4,)),
             pltpu.SemaphoreType.DMA((3 + ITERS,)),
             pltpu.SemaphoreType.DMA((3 + ITERS,)),
-            pltpu.SemaphoreType.DMA((2 * ITERS, 8)),
-            pltpu.SemaphoreType.DMA((2 * ITERS, 8)),
+            pltpu.SemaphoreType.DMA((HALOS, 10)),
+            pltpu.SemaphoreType.DMA((HALOS, 10)),
             pltpu.SemaphoreType.DMA((ITERS, 2)),
             pltpu.SemaphoreType.DMA((ITERS, 2)),
             pltpu.SemaphoreType.DMA((ITERS, 2)),

time: 76.4 us -> 70.7 us (0.925)
  Pallas kernels: 72.6 us -> 66.9 us
    pallas_call x1, Pallas kernels: 72.6 us -> 66.9 us  [shards(): pl.pallas_call(functools.partial(body, nf, nr, frames), out_shape=(out, o...]
where the time goes in v2:
time: 70.7 us; the launch traced here: 70.6 us
  Pallas kernels  66.9 us (95%)
  other arithmetic  2.35 us (3%)
    pallas_call x1, Pallas kernels, shards(): pl.pallas_call(functools.partial(body, nf, nr, frames), out_shape=(out, o...  66.9 us
    add x1, other arithmetic, shards(): return (spikes, spikes + beta * (spikes - first))  2.35 us

profile of v2, /device:TPU:1, one launch (start us, length us, event | category | flops | bytes accessed | tf_op | source)
XLA Modules:
  0.0 70.6 jit_solution(12880664648832764583)
XLA Ops:
  0.6 66.9 %fista.1 = (f32[4,2,8,2048]{3,2,1,0:T(8,128)}, f32[4,2,8,2048]{3,2,1,0:T(8,128)}, f32[1,128]{1,0:T(1,128)}) custom-call(bf16[4,2,8,2048]{3,2,1,0:T(8,128)(2,1)} %bitcast.27, bf16[127,2,8,128]{3,2,1,0:T(8,128)(2,1)} %bitcast.26, f32[4,2,8,2048]{3,2,1,0:T(8,128)} %bitcast.25, bf16[1,128]{1,0:T(2,128)(2,1)} %bitcast.28, f32[8]{0:T(128)} %half_hbm.1), custom_call_target="tpu_custom_call" | custom-call | tf_op jit(solution)/shard_map/fista/pallas_call | solution.py:652
  67.5 0.0 copy-start
  67.5 0.7 copy-done
  68.2 2.4 %fusion.3 = (f32[4,1,16,2048]{3,2,1,0:T(8,128)}, f32[4,1,16,2048]{3,2,1,0:T(8,128)}) fusion(f32[4,2,8,2048]{3,2,1,0:T(8,128)} %get-tuple-element.5, f32[]{:T(128)S(6)} %mul.41, f32[4,2,8,2048]{3,2,1,0:T(8,128)} %get-tuple-element.7, f32[]{:T(128)S(1)} %bitcast.30), kind=kLoop, calls=%fused_computation.5 | loop fusion | flops 917504 | bytes 2097160 | tf_op jit(solution)/shard_map/add | solution.py:718
Async XLA Ops:
  67.5 0.7 copy-start

commit v3 on v2

--- a/solution.py
+++ b/solution.py
@@ -444,7 +444,7 @@
                 extra = [2.0 * extra[g] if g in kept else gone for g in range(GROUPS)]
             return flat[block * rows : (block + 1) * rows] + jnp.concatenate(extra, axis=0)
 
-        return along_rows([part(0, 0, 1), part(1, 1, 0), part(2, 1, 1), part(3, 2, 0)])
+        return along_rows([part(0, 0, 1), part(1, 1, 0), part(2, 1, 1), part(3, 2, 0)], n in CURVATURE)
 
     def smooth_wide(it, buffer):
         blocks = [above_f[it], buffer[:, :, 0], buffer[:, :, 1], below_f[it]]
@@ -471,7 +471,7 @@
         blocks = [flat[b * rows : (b + 1) * rows] for b in range(4)]
         pull_f[it] = REG_WEIGHT * (field - along_rows(blocks))
 
-    def along_rows(blocks):
+    def along_rows(blocks, coarse=False):
         pairs = [split(b) for b in blocks]
         result = []
         for q in range(rows // rg):
@@ -486,8 +486,9 @@
                     axis=0,
                 )
 
-            high, low = tower(0), tower(1)
-            result.append(dot(ah[...], high) + dot(ah[...], low) + dot(al[...], high))
+            high = tower(0)
+            value = dot(ah[...], high) + dot(al[...], high)
+            result.append(value if coarse else value + dot(ah[...], tower(1)))
         return jnp.concatenate(result, axis=0) * scale
 
     lane = iota((1, 128), 1)
@@ -649,6 +650,7 @@
     any_spec = pl.BlockSpec(memory_space=pltpu.MemorySpace.HBM)
     vmem = pl.BlockSpec(memory_space=pltpu.VMEM)
     out = jax.ShapeDtypeStruct((per, 2, 8, cols), F32)
+    held = functools.partial(pltpu.with_memory_space_constraint, memory_space=pltpu.MemorySpace.HBM)
     first, slope, step = pl.pallas_call(
         functools.partial(body, nf, nr, frames),
         out_shape=(out, out, jax.ShapeDtypeStruct((1, 128), F32)),
@@ -700,15 +702,15 @@
             pltpu.SemaphoreType.DMA((ITERS, 2)),
         ],
         compiler_params=pltpu.CompilerParams(
-            collective_id=0, has_side_effects=True, vmem_limit_bytes=67043328
+            collective_id=0, has_side_effects=True, vmem_limit_bytes=44 * 1024 * 1024
         ),
         name="fista",
     )(
-        observed.reshape(per, 2, 8, cols),
-        history.reshape(hist, 2, 8, 128),
-        spikes_start.reshape(per, 2, 8, cols),
-        kernel.reshape(1, -1),
-        smooth_half,
+        held(observed.reshape(per, 2, 8, cols)),
+        held(history.reshape(hist, 2, 8, 128)),
+        held(spikes_start.reshape(per, 2, 8, cols)),
+        held(kernel.reshape(1, -1)),
+        held(smooth_half),
     )
     shape = spikes_start.shape
     step = step[0, 0]

time: 70.7 us -> 67.8 us (0.959)
  other arithmetic: 2.35 us -> 1.16 us
  Pallas kernels: 66.9 us -> 65.9 us
    add x1, other arithmetic: 2.35 us -> 1.16 us  [shards(): return (spikes, spikes + beta * (spikes - first))]
    pallas_call x1, Pallas kernels: 66.9 us -> 65.9 us  [shards(): pl.pallas_call(functools.partial(body, nf, nr, frames), out_shape=(out, o...]
where the time goes in v3:
time: 67.8 us; the launch traced here: 67.7 us
  Pallas kernels  65.9 us (97%)
  other arithmetic  1.16 us (2%)
    pallas_call x1, Pallas kernels, shards(): pl.pallas_call(functools.partial(body, nf, nr, frames), out_shape=(out, o...  65.9 us

profile of v3, /device:TPU:1, one launch (start us, length us, event | category | flops | bytes accessed | tf_op | source)
XLA Modules:
  0.0 67.7 jit_solution(14244231829638128455)
XLA Ops:
  0.6 65.9 %fista.1 = (f32[4,2,8,2048]{3,2,1,0:T(8,128)S(1)}, f32[4,2,8,2048]{3,2,1,0:T(8,128)S(1)}, f32[1,128]{1,0:T(1,128)S(1)}) custom-call(bf16[4,2,8,2048]{3,2,1,0:T(8,128)(2,1)} %bitcast.29, bf16[127,2,8,128]{3,2,1,0:T(8,128)(2,1)} %bitcast.28, f32[4,2,8,2048]{3,2,1,0:T(8,128)} %bitcast.27, bf16[1,128]{1,0:T(2,128)(2,1)} %bitcast.30, f32[8]{0:T(128)} %half_hbm.1), custom_call_target="tpu_custom_call" | custom-call | tf_op jit(solution)/shard_map/fista/pallas_call | solution.py:654
  66.6 1.2 %fusion.3 = (f32[4,1,16,2048]{3,2,1,0:T(8,128)}, f32[4,1,16,2048]{3,2,1,0:T(8,128)}) fusion(f32[4,2,8,2048]{3,2,1,0:T(8,128)S(1)} %get-tuple-element.5, f32[]{:T(128)S(6)} %mul.41, f32[4,2,8,2048]{3,2,1,0:T(8,128)S(1)} %get-tuple-element.7, f32[]{:T(128)S(1)} %bitcast.26), kind=kLoop, calls=%fused_computation.5 | loop fusion | flops 917504 | bytes 2097160 | tf_op jit(solution)/shard_map/add | solution.py:720

commit v4 on v3

--- a/solution.py
+++ b/solution.py
@@ -412,11 +412,13 @@
     def halo_start(n, field):
         edge_s[n, 0] = field[:, 0:128]
         edge_s[n, 1] = field[:, 128:256]
+        copies = halo_copies(n)
+        start_all(copies[:2])
         wide = [field[g * chunk : (g + 1) * chunk, :] for g in range(GROUPS)]
         packed = dot(jnp.concatenate(wide, axis=1), sel[...]).astype(BF16)
         strip_s[n, 0] = packed[:, 0:128]
         strip_s[n, 1] = packed[:, 128:256]
-        start_all(halo_copies(n))
+        start_all(copies[2:])
 
     def smooth(n, field):
         if n in CURVATURE:

time: 67.8 us -> 67.3 us (level)
  no operation moved by 1% of the time
where the time goes in v4:
time: 67.3 us; the launch traced here: 67.2 us
  Pallas kernels  65.4 us (97%)
  other arithmetic  1.16 us (2%)
    pallas_call x1, Pallas kernels, shards(): pl.pallas_call(functools.partial(body, nf, nr, frames), out_shape=(out, o...  65.4 us

profile of v4, /device:TPU:1, one launch (start us, length us, event | category | flops | bytes accessed | tf_op | source)
XLA Modules:
  0.0 67.2 jit_solution(4416509300853368587)
XLA Ops:
  0.6 65.4 %fista.1 = (f32[4,2,8,2048]{3,2,1,0:T(8,128)S(1)}, f32[4,2,8,2048]{3,2,1,0:T(8,128)S(1)}, f32[1,128]{1,0:T(1,128)S(1)}) custom-call(bf16[4,2,8,2048]{3,2,1,0:T(8,128)(2,1)} %bitcast.29, bf16[127,2,8,128]{3,2,1,0:T(8,128)(2,1)} %bitcast.28, f32[4,2,8,2048]{3,2,1,0:T(8,128)} %bitcast.27, bf16[1,128]{1,0:T(2,128)(2,1)} %bitcast.30, f32[8]{0:T(128)} %half_hbm.1), custom_call_target="tpu_custom_call" | custom-call | tf_op jit(solution)/shard_map/fista/pallas_call | solution.py:656
  66.0 1.2 %fusion.3 = (f32[4,1,16,2048]{3,2,1,0:T(8,128)}, f32[4,1,16,2048]{3,2,1,0:T(8,128)}) fusion(f32[4,2,8,2048]{3,2,1,0:T(8,128)S(1)} %get-tuple-element.5, f32[]{:T(128)S(6)} %mul.41, f32[4,2,8,2048]{3,2,1,0:T(8,128)S(1)} %get-tuple-element.7, f32[]{:T(128)S(1)} %bitcast.26), kind=kLoop, calls=%fused_computation.5 | loop fusion | flops 917504 | bytes 2097160 | tf_op jit(solution)/shard_map/add | solution.py:722

commit v5 on v4

--- a/solution.py
+++ b/solution.py
@@ -420,7 +420,7 @@
         strip_s[n, 1] = packed[:, 128:256]
         start_all(copies[2:])
 
-    def smooth(n, field):
+    def along_columns(n, field):
         if n in CURVATURE:
             cut = rows // 2
             gone, twice = jnp.zeros((cut, 128), BF16), jnp.asarray(2.0, BF16)
@@ -446,7 +446,28 @@
                 extra = [2.0 * extra[g] if g in kept else gone for g in range(GROUPS)]
             return flat[block * rows : (block + 1) * rows] + jnp.concatenate(extra, axis=0)
 
-        return along_rows([part(0, 0, 1), part(1, 1, 0), part(2, 1, 1), part(3, 2, 0)], n in CURVATURE)
+        return [part(0, 0, 1), part(1, 1, 0), part(2, 1, 1), part(3, 2, 0)]
+
+    def smooth(n, field):
+        return along_rows(along_columns(n, field))
+
+    def rows_transposed(field):
+        result = []
+        for q in range(rows // rg):
+            tile = field[q * rg : (q + 1) * rg]
+            up, same, down = (
+                dot(ah[:, d * rg : (d + 1) * rg], tile) + dot(al[:, d * rg : (d + 1) * rg], tile)
+                for d in range(3)
+            )
+            result.append(
+                (
+                    down[:, 0:128],
+                    same[:, 0:128] + down[:, 128:256],
+                    up[:, 0:128] + same[:, 128:256],
+                    up[:, 128:256],
+                )
+            )
+        return [jnp.concatenate(parts, axis=0) for parts in zip(*result)]
 
     def smooth_wide(it, buffer):
         blocks = [above_f[it], buffer[:, :, 0], buffer[:, :, 1], below_f[it]]
@@ -473,7 +494,7 @@
         blocks = [flat[b * rows : (b + 1) * rows] for b in range(4)]
         pull_f[it] = REG_WEIGHT * (field - along_rows(blocks))
 
-    def along_rows(blocks, coarse=False):
+    def along_rows(blocks):
         pairs = [split(b) for b in blocks]
         result = []
         for q in range(rows // rg):
@@ -490,7 +511,7 @@
 
             high = tower(0)
             value = dot(ah[...], high) + dot(al[...], high)
-            result.append(value if coarse else value + dot(ah[...], tower(1)))
+            result.append(value + dot(ah[...], tower(1)))
         return jnp.concatenate(result, axis=0) * scale
 
     lane = iota((1, 128), 1)
@@ -587,12 +608,15 @@
             halo_start(4, (gradient - grad_bf.astype(F32)).astype(BF16))
         conv = dot(kw[...], grad_bf)
         norm, conv = total_of(gradient * gradient), total_of(conv * conv)
+        left = rows_transposed(grad_bf)
         if it == 1:
             store_first = update_first(steps[0])
         recv_all(halo_copies(2 * it + 1))
-        grad_smooth = smooth(2 * it + 1, grad_bf)
-        grad_f32 = grad_bf.astype(F32)
-        curv = total_of(grad_f32 * (grad_f32 - grad_smooth))
+        right = along_columns(2 * it + 1, grad_bf)
+        cross = sum(a * b for a, b in zip(left, right))
+        square = grad_bf.astype(F32)
+        square = square * square
+        curv = total_of(square[:, 0:128] + square[:, 128:256] - scale * cross)
         sum_start(it, 0, jnp.where(lane == 0, norm, jnp.where(lane == 1, conv, curv)))
         if it == 0:
             wait_bytes(lo_c, a2a_recv.at[2])

time: 67.3 us -> 66.4 us (0.987)
  Pallas kernels: 65.4 us -> 64.5 us
    pallas_call x1, Pallas kernels: 65.4 us -> 64.5 us  [shards(): pl.pallas_call(functools.partial(body, nf, nr, frames), out_shape=(out, o...]
where the time goes in v5:
time: 66.4 us; the launch traced here: 66.3 us
  Pallas kernels  64.5 us (97%)
  other arithmetic  1.16 us (2%)
  between operations  0.67 us (1%)
    pallas_call x1, Pallas kernels, shards(): pl.pallas_call(functools.partial(body, nf, nr, frames), out_shape=(out, o...  64.5 us

profile of v5, /device:TPU:1, one launch (start us, length us, event | category | flops | bytes accessed | tf_op | source)
XLA Modules:
  0.0 66.3 jit_solution(9943314482335417285)
XLA Ops:
  0.6 64.5 %fista.1 = (f32[4,2,8,2048]{3,2,1,0:T(8,128)S(1)}, f32[4,2,8,2048]{3,2,1,0:T(8,128)S(1)}, f32[1,128]{1,0:T(1,128)S(1)}) custom-call(bf16[4,2,8,2048]{3,2,1,0:T(8,128)(2,1)} %bitcast.29, bf16[127,2,8,128]{3,2,1,0:T(8,128)(2,1)} %bitcast.28, f32[4,2,8,2048]{3,2,1,0:T(8,128)} %bitcast.27, bf16[1,128]{1,0:T(2,128)(2,1)} %bitcast.30, f32[8]{0:T(128)} %half_hbm.1), custom_call_target="tpu_custom_call" | custom-call | tf_op jit(solution)/shard_map/fista/pallas_call | solution.py:680
  65.2 1.2 %fusion.3 = (f32[4,1,16,2048]{3,2,1,0:T(8,128)}, f32[4,1,16,2048]{3,2,1,0:T(8,128)}) fusion(f32[4,2,8,2048]{3,2,1,0:T(8,128)S(1)} %get-tuple-element.5, f32[]{:T(128)S(6)} %mul.41, f32[4,2,8,2048]{3,2,1,0:T(8,128)S(1)} %get-tuple-element.7, f32[]{:T(128)S(1)} %bitcast.26), kind=kLoop, calls=%fused_computation.5 | loop fusion | flops 917504 | bytes 2097160 | tf_op jit(solution)/shard_map/add | solution.py:746

commit v6 on v5

--- a/solution.py
+++ b/solution.py
@@ -420,18 +420,22 @@
         strip_s[n, 1] = packed[:, 128:256]
         start_all(copies[2:])
 
-    def along_columns(n, field):
+    def columns_inside(stacked):
+        wide = dot(stacked, band[128:256])
+        return wide[:, 0:128] + wide[:, 128:256]
+
+    def own_columns(field):
+        return columns_inside(jnp.concatenate([field[:, 0:128], field[:, 128:256]], axis=0))
+
+    def along_columns(n, own):
         if n in CURVATURE:
             cut = rows // 2
             gone, twice = jnp.zeros((cut, 128), BF16), jnp.asarray(2.0, BF16)
             outer = [above[n, 0:cut] * twice, gone], [gone, below[n, cut:rows] * twice]
         else:
             outer = [above[n]], [below[n]]
-        stacked = jnp.concatenate(
-            [*outer[0], field[:, 0:128], field[:, 128:256], *outer[1]], axis=0
-        )
-        wide = dot(stacked, band[128:256])
-        flat = wide[:, 0:128] + wide[:, 128:256]
+        outside = columns_inside(jnp.concatenate([*outer[0], *outer[1]], axis=0))
+        flat = jnp.concatenate([outside[:rows], own, outside[rows:]], axis=0)
         lines = strips[n].reshape(3 * chunk, 256)
         corner = dot(lines, hbh[...]) + dot(lines, hbl[...])
 
@@ -449,7 +453,7 @@
         return [part(0, 0, 1), part(1, 1, 0), part(2, 1, 1), part(3, 2, 0)]
 
     def smooth(n, field):
-        return along_rows(along_columns(n, field))
+        return along_rows(along_columns(n, own_columns(field)))
 
     def rows_transposed(field):
         result = []
@@ -609,10 +613,11 @@
         conv = dot(kw[...], grad_bf)
         norm, conv = total_of(gradient * gradient), total_of(conv * conv)
         left = rows_transposed(grad_bf)
+        own = own_columns(grad_bf)
         if it == 1:
             store_first = update_first(steps[0])
         recv_all(halo_copies(2 * it + 1))
-        right = along_columns(2 * it + 1, grad_bf)
+        right = along_columns(2 * it + 1, own)
         cross = sum(a * b for a, b in zip(left, right))
         square = grad_bf.astype(F32)
         square = square * square

time: 66.4 us -> 65.8 us (level)
  no operation moved by 1% of the time
where the time goes in v6:
time: 65.8 us; the launch traced here: 65.7 us
  Pallas kernels  63.9 us (97%)
  other arithmetic  1.16 us (2%)
  between operations  0.67 us (1%)
    pallas_call x1, Pallas kernels, shards(): pl.pallas_call(functools.partial(body, nf, nr, frames), out_shape=(out, o...  63.9 us

profile of v6, /device:TPU:1, one launch (start us, length us, event | category | flops | bytes accessed | tf_op | source)
XLA Modules:
  0.0 65.7 jit_solution(16065231361736203518)
XLA Ops:
  0.6 63.9 %fista.1 = (f32[4,2,8,2048]{3,2,1,0:T(8,128)S(1)}, f32[4,2,8,2048]{3,2,1,0:T(8,128)S(1)}, f32[1,128]{1,0:T(1,128)S(1)}) custom-call(bf16[4,2,8,2048]{3,2,1,0:T(8,128)(2,1)} %bitcast.29, bf16[127,2,8,128]{3,2,1,0:T(8,128)(2,1)} %bitcast.28, f32[4,2,8,2048]{3,2,1,0:T(8,128)} %bitcast.27, bf16[1,128]{1,0:T(2,128)(2,1)} %bitcast.30, f32[8]{0:T(128)} %half_hbm.1), custom_call_target="tpu_custom_call" | custom-call | tf_op jit(solution)/shard_map/fista/pallas_call | solution.py:685
  64.6 1.2 %fusion.3 = (f32[4,1,16,2048]{3,2,1,0:T(8,128)}, f32[4,1,16,2048]{3,2,1,0:T(8,128)}) fusion(f32[4,2,8,2048]{3,2,1,0:T(8,128)S(1)} %get-tuple-element.5, f32[]{:T(128)S(6)} %mul.41, f32[4,2,8,2048]{3,2,1,0:T(8,128)S(1)} %get-tuple-element.7, f32[]{:T(128)S(1)} %bitcast.26), kind=kLoop, calls=%fused_computation.5 | loop fusion | flops 917504 | bytes 2097160 | tf_op jit(solution)/shard_map/add | solution.py:751
